TPU v7x, 256 devices: a whole 4x4x8 slice. The times are simulated.
256 devices in a mesh: section: 64 (over y, z, core), dp: 4 (over x).
Axes of the slice: x: 4, y: 4, z: 8, core: 2. Of those that a mesh axis runs over, the one named last changes fastest.
Arguments:
- tokens: bfloat16 [1024, 8192], P(('section', 'dp')), may hold values from -6 to 6
- norm_gain: float32 [8192], replicated, may hold values from 0.1 to 1.9
- gate_weight: bfloat16 [8192, 28672], P('dp', 'section'), may hold values from -0.0625 to 0.0625
- up_weight: bfloat16 [8192, 28672], P('dp', 'section'), may hold values from -0.0625 to 0.0625
- down_weight: bfloat16 [28672, 8192], P('section', 'dp'), may hold values from -0.03125 to 0.03125
Outputs:
- mixed: bfloat16 [1024, 8192], P(('section', 'dp'))
All inputs are finite; a program needn't handle non-finite values.
Results may differ from a plain program's by a relative error of at most 0.0046.
Values may be sent and summed in bfloat16 or wider, within the bound.
No kernel may reach another device: no remote copies, remote signals or barrier semaphores. Data moves between devices by JAX's collectives and lax.ppermute only.
A program may use at most 128 MiB of HBM per device.

v0:
```python
import jax
import jax.numpy as jnp
from jax import lax
from jax.sharding import PartitionSpec as P


def local(tokens, norm_gain, gate_weight, up_weight, down_weight):
    widened = tokens.astype(jnp.float32)
    mean_square = jnp.mean(widened * widened, axis=1, keepdims=True)
    normed_own = (widened * lax.rsqrt(mean_square + 1e-05) * norm_gain[None, :]).astype(
        jnp.bfloat16
    )
    normed = lax.all_gather(normed_own, "section", axis=0, tiled=True)
    full_gate, full_up, full_down = (
        lax.all_gather(gate_weight, "dp", axis=0, tiled=True),
        lax.all_gather(up_weight, "dp", axis=0, tiled=True),
        lax.all_gather(down_weight, "dp", axis=1, tiled=True),
    )
    gate_part = jnp.dot(normed, full_gate, preferred_element_type=jnp.float32)
    up_part = jnp.dot(normed, full_up, preferred_element_type=jnp.float32)
    hidden = (jax.nn.silu(gate_part) * up_part).astype(jnp.bfloat16)
    summed = lax.psum_scatter(
        jnp.dot(hidden, full_down, preferred_element_type=jnp.float32),
        "section",
        scatter_dimension=0,
        tiled=True,
    )
    return (widened + summed).astype(jnp.bfloat16)


def solution(mesh):
    return jax.shard_map(
        local,
        mesh=mesh,
        in_specs=(
            P(("section", "dp"), None),
            P(),
            P("dp", "section"),
            P("dp", "section"),
            P("section", "dp"),
        ),
        out_specs=P(("section", "dp"), None),
        check_vma=False,
    )
```

profile of v0, /device:TPU:2, one launch (start us, length us, event | category | flops | bytes accessed | tf_op | source)
XLA Modules:
  0.0 550.5 jit_solution(717318222495191974)
XLA Ops:
  6.5 1.0 fusion.1
  7.6 1.6 fusion.5
  9.1 0.0 all-gather.12.cloned.1.call-update
  9.2 0.0 all-gather.6.cloned.1.call-start
  9.2 0.7 all-gather.6.cloned.1.call-update
  9.9 0.0 all-gather.8.cloned.1.call-start
  10.0 0.7 all-gather.8.cloned.1.call-update
  10.7 0.0 all-gather.10.cloned.1.call-start
  10.7 0.5 all-gather.10.cloned.1.call-update
  11.2 0.0 all-reduce.3.cloned.1.call-start
  11.3 80.9 %all-gather.12.cloned.1.call-done = bf16[64,4,8192]{2,1,0:T(4,128)(2,1)} async-done(((bf16[1,4,8192]{2,1,0:T(4,128)(2,1)}), bf16[64,4,8192]{2,1,0:T(4,128)(2,1)}) %all-gather.12.cloned.1.call-update) | async-done | bytes 4194320 | tf_op jit(solution)/shard_map/all_gather | solution.py:13
  92.2 6.9 %reshape.10 = bf16[256,8192]{1,0:T(8,128)(2,1)} reshape(bf16[64,4,8192]{2,1,0:T(4,128)(2,1)} %all-gather.12.cloned.1.call-done) | data formatting | bytes 8388608
  99.1 69.0 %all-gather.6.cloned.1.call-done = bf16[8192,448]{0,1:T(8,128)(2,1)} async-done(((bf16[2048,448]{0,1:T(8,128)(2,1)}), bf16[8192,448]{0,1:T(8,128)(2,1)}) %all-gather.6.cloned.1.call-update) | async-done | bytes 7340048 | tf_op jit(solution)/shard_map/all_gather | solution.py:15
  168.1 6.4 %fusion.6 = f32[256,448]{0,1:T(8,128)S(1)} fusion(bf16[256,8192]{1,0:T(8,128)(2,1)} %reshape.10, bf16[8192,448]{0,1:T(8,128)(2,1)} %all-gather.6.cloned.1.call-done), kind=kOutput, calls=%fused_computation.11 | convolution fusion | flops 1879048192 | bytes 11993088 | tf_op jit(solution)/shard_map/dot_general | solution.py:19
  174.5 73.2 %all-gather.8.cloned.1.call-done = bf16[8192,448]{0,1:T(8,128)(2,1)} async-done(((bf16[2048,448]{0,1:T(8,128)(2,1)}), bf16[8192,448]{0,1:T(8,128)(2,1)}) %all-gather.8.cloned.1.call-update) | async-done | bytes 7340048 | tf_op jit(solution)/shard_map/all_gather | solution.py:16
  247.7 6.5 %fusion = bf16[256,448]{0,1:T(8,128)(2,1)S(1)} fusion(bf16[256,8192]{1,0:T(8,128)(2,1)} %reshape.10, bf16[8192,448]{0,1:T(8,128)(2,1)} %all-gather.8.cloned.1.call-done, f32[256,448]{0,1:T(8,128)S(1)} %fusion.6), kind=kOutput, calls=%fused_computation.1 | convolution fusion | flops 1879736320 | bytes 12222464 | tf_op jit(solution)/shard_map/dot_general | solution.py:20
  254.2 73.0 %all-gather.10.cloned.1.call-done = bf16[448,8192]{1,0:T(8,128)(2,1)} async-done(((bf16[448,2048]{1,0:T(8,128)(2,1)}), bf16[448,8192]{1,0:T(8,128)(2,1)}) %all-gather.10.cloned.1.call-update) | async-done | bytes 7340048 | tf_op jit(solution)/shard_map/all_gather | solution.py:17
  327.2 8.8 %fusion.7 = f32[256,8192]{1,0:T(8,128)} fusion(bf16[256,448]{0,1:T(8,128)(2,1)S(1)} %fusion, bf16[448,8192]{1,0:T(8,128)(2,1)} %all-gather.10.cloned.1.call-done), kind=kOutput, calls=%fused_computation.12 | convolution fusion | flops 1879048192 | bytes 15958016 | tf_op jit(solution)/shard_map/dot_general | solution.py:23
  336.0 0.0 all-reduce.3.cloned.1.call-update
  336.0 0.6 copy-done.1
  336.6 0.6 dynamic-slice
  337.9 204.5 %all-reduce.3.cloned.1.call-done = f32[256,8192]{1,0:T(8,128)} async-done(((f32[256,8192]{1,0:T(8,128)}), f32[256,8192]{1,0:T(8,128)}) %all-reduce.3.cloned.1.call-update) | async-done | bytes 8388624
  542.4 0.0 copy-done
  542.4 1.6 fusion.4
  (4 shorter events, 0.0 us)
Async XLA Ops:
  6.5 85.6 %all-gather.12.cloned.1.call-start = ((), (), s32[]{:S(2)}) async-start(), calls=%async_computation.3 | async-start | bytes 4259840 | tf_op jit(solution)/shard_map/all_gather | solution.py:13
  9.2 158.9 %all-gather.6.cloned.1.call-start = ((), (), s32[]{:S(2)}) async-start(), calls=%async_computation | async-start | bytes 9175040 | tf_op jit(solution)/shard_map/all_gather | solution.py:15
  9.9 237.8 %all-gather.8.cloned.1.call-start = ((), (), s32[]{:S(2)}) async-start(), calls=%async_computation.1 | async-start | bytes 9175040 | tf_op jit(solution)/shard_map/all_gather | solution.py:16
  10.7 316.5 %all-gather.10.cloned.1.call-start = ((), (), s32[]{:S(2)}) async-start(), calls=%async_computation.2 | async-start | bytes 9175040 | tf_op jit(solution)/shard_map/all_gather | solution.py:17
  11.2 531.1 %all-reduce.3.cloned.1.call-start = ((), (), s32[]{:S(2)}) async-start(), calls=%async_computation.4 | async-start | bytes 16777216
  336.0 0.7 copy-start.1
  336.0 206.4 %copy-start = (bf16[4,8192]{1,0:T(4,128)(2,1)S(1)}, bf16[4,8192]{1,0:T(4,128)(2,1)}, u32[]{:S(2)}) copy-start(bf16[4,8192]{1,0:T(4,128)(2,1)} %param.5) | copy-start | bytes 196612
Sparse Core Ops, SparseCore 0:
  10.1 81.9 all-gather.11
  94.0 74.0 all-gather.5
  169.9 77.7 all-gather.7
  249.4 77.7 all-gather.9
  336.1 206.2 all-reduce.2
where the time goes:
time: 551 us
  waiting for transfers between devices  503 us (91%)
  matrix products  21.7 us (4%)
  between operations  13.8 us (3%)
  local copies, waits for them, and re-layouts  8.13 us (1%)
    unnamed x6, waiting for transfers between devices  206 us
    all_gather x1, waiting for transfers between devices, local(): normed = lax.all_gather(normed_own, 'section', axis=0, tiled=True)  80.9 us
    all_gather x1, waiting for transfers between devices, local(): lax.all_gather(up_weight, 'dp', axis=0, tiled=True)  73.2 us
    all_gather x1, waiting for transfers between devices, local(): lax.all_gather(down_weight, 'dp', axis=1, tiled=True)  73 us
    all_gather x1, waiting for transfers between devices, local(): lax.all_gather(gate_weight, 'dp', axis=0, tiled=True)  69 us
  transfers between devices with their start and end apart: 5, of which 5 were waited for; matrix products, arithmetic and copies ran while one was open for 4% of the time, Pallas kernels for 0%

commit v1 on v0

--- a/solution.py
+++ b/solution.py
@@ -2,6 +2,7 @@
 import jax.numpy as jnp
 from jax import lax
 from jax.sharding import PartitionSpec as P
+from jax.lax import all_to_all, axis_size
 
 
 def local(tokens, norm_gain, gate_weight, up_weight, down_weight):
@@ -10,7 +11,12 @@
     normed_own = (widened * lax.rsqrt(mean_square + 1e-05) * norm_gain[None, :]).astype(
         jnp.bfloat16
     )
-    normed = lax.all_gather(normed_own, "section", axis=0, tiled=True)
+    normed = jnp.concatenate(
+        all_to_all(
+            jnp.stack([normed_own for _ in range(axis_size("section"))], axis=0), "section", 0, 0
+        ),
+        axis=0,
+    )
     full_gate, full_up, full_down = (
         lax.all_gather(gate_weight, "dp", axis=0, tiled=True),
         lax.all_gather(up_weight, "dp", axis=0, tiled=True),

time: 551 us -> 472 us (0.86)
  waiting for transfers between devices: 503 us -> 314 us
  blocking collectives: 0 us -> 108 us
    all_to_all x0 -> x1, blocking collectives: none -> 108 us  [local(): all_to_all(jnp.stack([normed_own for _ in range(axis_size('section'))], a...]
    all_gather x1 -> x0, waiting for transfers between devices: 80.9 us -> none  [local(): normed = lax.all_gather(normed_own, 'section', axis=0, tiled=True)]
    all_gather x1, waiting for transfers between devices: 69 us -> 0.01 us  [local(): lax.all_gather(gate_weight, 'dp', axis=0, tiled=True)]
    all_gather x1, waiting for transfers between devices: 73.2 us -> 34.1 us  [local(): lax.all_gather(up_weight, 'dp', axis=0, tiled=True)]
    reshape x0 -> x1, local copies, waits for them, and re-layouts: none -> 6.96 us  [local(): jnp.concatenate(all_to_all(jnp.stack([normed_own for _ in range(axis_size...]
    unnamed x6 -> x5, local copies, waits for them, and re-layouts: 8.13 us -> 1.23 us
    unnamed x6 -> x5, waiting for transfers between devices: 206 us -> 207 us
  transfers between devices with their start and end apart: 5 -> 4, of which waited for: 5 -> 3; matrix products, arithmetic and copies ran while one was open for 4% -> 5% of each run, Pallas kernels for 0% -> 0%
where the time goes in v1:
time: 472 us
  waiting for transfers between devices  314 us (67%)
  blocking collectives  108 us (23%)
  matrix products  21.8 us (5%)
  between operations  13.8 us (3%)
  local copies, waits for them, and re-layouts  10.2 us (2%)
    unnamed x5, waiting for transfers between devices  207 us
    all_to_all x1, blocking collectives, local(): all_to_all(jnp.stack([normed_own for _ in range(axis_size('section'))], a...  108 us
    all_gather x1, waiting for transfers between devices, local(): lax.all_gather(down_weight, 'dp', axis=1, tiled=True)  73.2 us
    all_gather x1, waiting for transfers between devices, local(): lax.all_gather(up_weight, 'dp', axis=0, tiled=True)  34.1 us
  transfers between devices with their start and end apart: 4, of which 3 were waited for; matrix products, arithmetic and copies ran while one was open for 5% of the time, Pallas kernels for 0%

profile of v1, /device:TPU:2, one launch (start us, length us, event | category | flops | bytes accessed | tf_op | source)
XLA Modules:
  0.0 471.5 jit_solution(16459609966912231522)
XLA Ops:
  6.5 0.0 all-gather.4.cloned.1.call-start
  6.5 0.7 all-gather.4.cloned.1.call-update
  7.3 0.0 all-gather.6.cloned.1.call-start
  7.3 0.7 all-gather.6.cloned.1.call-update
  8.0 0.0 all-gather.8.cloned.1.call-start
  8.1 0.7 all-gather.8.cloned.1.call-update
  8.7 0.0 all-reduce.3.cloned.1.call-start
  8.8 1.0 fusion.1
  9.8 0.9 fusion.3
  10.8 2.0 stack.2
  12.8 108.1 %all_to_all.5 = bf16[64,4,8192]{2,1,0:T(4,128)(2,1)} all-to-all(bf16[64,4,8192]{2,1,0:T(4,128)(2,1)S(1)} %stack.2), channel_id=1, replica_groups=mesh['section'=64,'dp'=4] {'section'}, dimensions={0} | all-to-all | bytes 8388608 | tf_op jit(solution)/shard_map/all_to_all | solution.py:15
  120.9 7.0 %reshape.14 = bf16[256,8192]{1,0:T(8,128)(2,1)} reshape(bf16[64,4,8192]{2,1,0:T(4,128)(2,1)} %all_to_all.5) | data formatting | bytes 8388608 | tf_op jit(solution)/shard_map/reshape | solution.py:14
  127.9 0.0 all-gather.4.cloned.1.call-done
  127.9 6.6 %fusion.5 = f32[256,448]{0,1:T(8,128)S(1)} fusion(bf16[256,8192]{1,0:T(8,128)(2,1)} %reshape.14, bf16[8192,448]{0,1:T(8,128)(2,1)} %all-gather.4.cloned.1.call-done), kind=kOutput, calls=%fused_computation.10 | convolution fusion | flops 1879048192 | bytes 11993088 | tf_op jit(solution)/shard_map/dot_general | solution.py:25
  134.5 34.1 %all-gather.6.cloned.1.call-done = bf16[8192,448]{0,1:T(8,128)(2,1)} async-done(((bf16[2048,448]{0,1:T(8,128)(2,1)}), bf16[8192,448]{0,1:T(8,128)(2,1)}) %all-gather.6.cloned.1.call-update) | async-done | bytes 7340048 | tf_op jit(solution)/shard_map/all_gather | solution.py:22
  168.6 6.4 %fusion = bf16[256,448]{0,1:T(8,128)(2,1)S(1)} fusion(bf16[256,8192]{1,0:T(8,128)(2,1)} %reshape.14, bf16[8192,448]{0,1:T(8,128)(2,1)} %all-gather.6.cloned.1.call-done, f32[256,448]{0,1:T(8,128)S(1)} %fusion.5), kind=kOutput, calls=%fused_computation.1 | convolution fusion | flops 1879736320 | bytes 12222464 | tf_op jit(solution)/shard_map/dot_general | solution.py:26
  175.0 73.2 %all-gather.8.cloned.1.call-done = bf16[448,8192]{1,0:T(8,128)(2,1)} async-done(((bf16[448,2048]{1,0:T(8,128)(2,1)}), bf16[448,8192]{1,0:T(8,128)(2,1)}) %all-gather.8.cloned.1.call-update) | async-done | bytes 7340048 | tf_op jit(solution)/shard_map/all_gather | solution.py:23
  248.2 8.8 %fusion.6 = f32[256,8192]{1,0:T(8,128)} fusion(bf16[256,448]{0,1:T(8,128)(2,1)S(1)} %fusion, bf16[448,8192]{1,0:T(8,128)(2,1)} %all-gather.8.cloned.1.call-done), kind=kOutput, calls=%fused_computation.11 | convolution fusion | flops 1879048192 | bytes 15958016 | tf_op jit(solution)/shard_map/dot_general | solution.py:29
  257.0 0.0 all-reduce.3.cloned.1.call-update
  257.0 0.6 copy-done.1
  257.6 0.6 dynamic-slice
  258.9 204.5 %all-reduce.3.cloned.1.call-done = f32[256,8192]{1,0:T(8,128)} async-done(((f32[256,8192]{1,0:T(8,128)}), f32[256,8192]{1,0:T(8,128)}) %all-reduce.3.cloned.1.call-update) | async-done | bytes 8388624
  463.4 0.0 copy-done
  463.4 1.6 fusion.4
  (3 shorter events, 0.0 us)
Async XLA Ops:
  6.5 121.4 %all-gather.4.cloned.1.call-start = ((), (), s32[]{:S(2)}) async-start(), calls=%async_computation.1 | async-start | bytes 9175040 | tf_op jit(solution)/shard_map/all_gather | solution.py:21
  7.3 161.3 %all-gather.6.cloned.1.call-start = ((), (), s32[]{:S(2)}) async-start(), calls=%async_computation.2 | async-start | bytes 9175040 | tf_op jit(solution)/shard_map/all_gather | solution.py:22
  8.0 240.2 %all-gather.8.cloned.1.call-start = ((), (), s32[]{:S(2)}) async-start(), calls=%async_computation.3 | async-start | bytes 9175040 | tf_op jit(solution)/shard_map/all_gather | solution.py:23
  8.7 454.6 %all-reduce.3.cloned.1.call-start = ((), (), s32[]{:S(2)}) async-start(), calls=%async_computation.4 | async-start | bytes 16777216
  257.0 0.7 copy-start.1
  257.0 206.4 %copy-start = (bf16[4,8192]{1,0:T(4,128)(2,1)S(1)}, bf16[4,8192]{1,0:T(4,128)(2,1)}, u32[]{:S(2)}) copy-start(bf16[4,8192]{1,0:T(4,128)(2,1)} %param.5) | copy-start | bytes 196612
Sparse Core Ops, SparseCore 0:
  9.2 79.7 all-gather.3
  90.7 77.7 all-gather.5
  170.4 77.7 all-gather.7
  257.1 206.2 all-reduce.2

commit v2 on v0

--- a/solution.py
+++ b/solution.py
@@ -11,10 +11,18 @@
         jnp.bfloat16
     )
     normed = lax.all_gather(normed_own, "section", axis=0, tiled=True)
+
+    def draw_ratios(values):
+        dev_count = lax.axis_size("dp")
+        queue = [dev_count if ix == 1 else 1 for ix in range(values.ndim)]
+        return lax.all_to_all(
+            jnp.tile(values, queue), axis_name="dp", split_axis=1, concat_axis=1, tiled=True
+        )
+
     full_gate, full_up, full_down = (
         lax.all_gather(gate_weight, "dp", axis=0, tiled=True),
         lax.all_gather(up_weight, "dp", axis=0, tiled=True),
-        lax.all_gather(down_weight, "dp", axis=1, tiled=True),
+        draw_ratios(down_weight),
     )
     gate_part = jnp.dot(normed, full_gate, preferred_element_type=jnp.float32)
     up_part = jnp.dot(normed, full_up, preferred_element_type=jnp.float32)

time: 551 us -> 478 us (0.87)
  waiting for transfers between devices: 503 us -> 333 us
  blocking collectives: 0 us -> 85.9 us
  local copies, waits for them, and re-layouts: 8.13 us -> 18.4 us
    all_to_all x0 -> x1, blocking collectives: none -> 85.9 us  [draw_ratios(): lax.all_to_all(jnp.tile(values, queue), axis_name='dp', split_axis=1, con...]
    all_gather x1, waiting for transfers between devices: 80.9 us -> 0.01 us  [local(): normed = lax.all_gather(normed_own, 'section', axis=0, tiled=True)]
    all_gather x1 -> x0, waiting for transfers between devices: 73 us -> none  [local(): lax.all_gather(down_weight, 'dp', axis=1, tiled=True)]
    all_gather x1, waiting for transfers between devices: 69 us -> 54.4 us  [local(): lax.all_gather(gate_weight, 'dp', axis=0, tiled=True)]
    unnamed x6 -> x5, waiting for transfers between devices: 206 us -> 206 us
  transfers between devices with their start and end apart: 5 -> 4, of which waited for: 5 -> 3; matrix products, arithmetic and copies ran while one was open for 4% -> 5% of each run, Pallas kernels for 0% -> 0%
where the time goes in v2:
time: 478 us; the launch traced here: 477 us
  waiting for transfers between devices  333 us (70%)
  blocking collectives  85.9 us (18%)
  matrix products  21.6 us (5%)
  local copies, waits for them, and re-layouts  18.4 us (4%)
  between operations  13.8 us (3%)
    unnamed x5, waiting for transfers between devices  206 us
    all_to_all x1, blocking collectives, draw_ratios(): lax.all_to_all(jnp.tile(values, queue), axis_name='dp', split_axis=1, con...  85.9 us
    all_gather x1, waiting for transfers between devices, local(): lax.all_gather(up_weight, 'dp', axis=0, tiled=True)  73.2 us
    all_gather x1, waiting for transfers between devices, local(): lax.all_gather(gate_weight, 'dp', axis=0, tiled=True)  54.4 us
  transfers between devices with their start and end apart: 4, of which 3 were waited for; matrix products, arithmetic and copies ran while one was open for 5% of the time, Pallas kernels for 0%

profile of v2, /device:TPU:2, one launch (start us, length us, event | category | flops | bytes accessed | tf_op | source)
XLA Modules:
  0.0 477.4 jit_solution(16485420358006319867)
XLA Ops:
  6.5 0.0 all-gather.9.cloned.1.call-start
  6.5 1.0 fusion.1
  7.6 1.6 fusion.5
  9.1 0.0 all-gather.9.cloned.1.call-update
  9.2 0.0 all-gather.5.cloned.1.call-start
  9.2 0.7 all-gather.5.cloned.1.call-update
  9.9 0.0 all-gather.7.cloned.1.call-start
  10.0 0.7 all-gather.7.cloned.1.call-update
  10.7 0.0 all-reduce.3.cloned.1.call-start
  10.7 5.4 %tile.2 = bf16[448,4,2048]{2,0,1:T(8,128)(2,1)} broadcast(bf16[448,2048]{1,0:T(8,128)(2,1)} %param.9), dimensions={0,2} | broadcast | bytes 9175040 | tf_op jit(solution)/shard_map/tile | solution.py:19
  16.1 85.9 %all_to_all.9 = bf16[448,4,2048]{2,0,1:T(8,128)(2,1)S(1)} all-to-all(bf16[448,4,2048]{2,0,1:T(8,128)(2,1)} %tile.2), channel_id=1, replica_groups=mesh['section'=64,'dp'=4] {'dp'}, dimensions={1} | all-to-all | bytes 14680064 | tf_op jit(solution)/shard_map/all_to_all | solution.py:18
  102.0 4.7 copy.7
  106.7 7.0 %reshape.17 = bf16[256,8192]{1,0:T(8,128)(2,1)} reshape(bf16[64,4,8192]{2,1,0:T(4,128)(2,1)} %all-gather.9.cloned.1.call-done) | data formatting | bytes 8388608
  113.7 54.4 %all-gather.5.cloned.1.call-done = bf16[8192,448]{0,1:T(8,128)(2,1)} async-done(((bf16[2048,448]{0,1:T(8,128)(2,1)}), bf16[8192,448]{0,1:T(8,128)(2,1)}) %all-gather.5.cloned.1.call-update) | async-done | bytes 7340048 | tf_op jit(solution)/shard_map/all_gather | solution.py:23
  168.1 6.4 %fusion.6 = f32[256,448]{0,1:T(8,128)S(1)} fusion(bf16[256,8192]{1,0:T(8,128)(2,1)} %reshape.17, bf16[8192,448]{0,1:T(8,128)(2,1)} %all-gather.5.cloned.1.call-done), kind=kOutput, calls=%fused_computation.11 | convolution fusion | flops 1879048192 | bytes 11993088 | tf_op jit(solution)/shard_map/dot_general | solution.py:27
  174.5 73.2 %all-gather.7.cloned.1.call-done = bf16[8192,448]{0,1:T(8,128)(2,1)} async-done(((bf16[2048,448]{0,1:T(8,128)(2,1)}), bf16[8192,448]{0,1:T(8,128)(2,1)}) %all-gather.7.cloned.1.call-update) | async-done | bytes 7340048 | tf_op jit(solution)/shard_map/all_gather | solution.py:24
  247.7 6.5 %fusion = bf16[256,448]{0,1:T(8,128)(2,1)S(1)} fusion(bf16[256,8192]{1,0:T(8,128)(2,1)} %reshape.17, bf16[8192,448]{0,1:T(8,128)(2,1)} %all-gather.7.cloned.1.call-done, f32[256,448]{0,1:T(8,128)S(1)} %fusion.6), kind=kOutput, calls=%fused_computation.1 | convolution fusion | flops 1879736320 | bytes 12222464 | tf_op jit(solution)/shard_map/dot_general | solution.py:28
  254.2 8.7 %fusion.7 = f32[256,8192]{1,0:T(8,128)} fusion(bf16[256,448]{0,1:T(8,128)(2,1)S(1)} %fusion, bf16[448,8192]{1,0:T(8,128)(2,1)} %bitcast.11), kind=kOutput, calls=%fused_computation.12 | convolution fusion | flops 1879048192 | bytes 15958016 | tf_op jit(solution)/shard_map/dot_general | solution.py:31
  262.9 0.0 all-reduce.3.cloned.1.call-update
  262.9 0.6 copy-done.1
  263.5 0.6 dynamic-slice
  264.8 204.5 %all-reduce.3.cloned.1.call-done = f32[256,8192]{1,0:T(8,128)} async-done(((f32[256,8192]{1,0:T(8,128)}), f32[256,8192]{1,0:T(8,128)}) %all-reduce.3.cloned.1.call-update) | async-done | bytes 8388624
  469.3 0.0 copy-done
  469.3 1.6 fusion.4
  (4 shorter events, 0.0 us)
Async XLA Ops:
  6.5 100.1 %all-gather.9.cloned.1.call-start = ((), (), s32[]{:S(2)}) async-start(), calls=%async_computation.3 | async-start | bytes 4259840 | tf_op jit(solution)/shard_map/all_gather | solution.py:13
  9.2 158.9 %all-gather.5.cloned.1.call-start = ((), (), s32[]{:S(2)}) async-start(), calls=%async_computation.1 | async-start | bytes 9175040 | tf_op jit(solution)/shard_map/all_gather | solution.py:23
  9.9 237.8 %all-gather.7.cloned.1.call-start = ((), (), s32[]{:S(2)}) async-start(), calls=%async_computation.2 | async-start | bytes 9175040 | tf_op jit(solution)/shard_map/all_gather | solution.py:24
  10.7 458.6 %all-reduce.3.cloned.1.call-start = ((), (), s32[]{:S(2)}) async-start(), calls=%async_computation.4 | async-start | bytes 16777216
  262.9 0.7 copy-start.1
  262.9 206.4 %copy-start = (bf16[4,8192]{1,0:T(4,128)(2,1)S(1)}, bf16[4,8192]{1,0:T(4,128)(2,1)}, u32[]{:S(2)}) copy-start(bf16[4,8192]{1,0:T(4,128)(2,1)} %param.5) | copy-start | bytes 196612
Sparse Core Ops, SparseCore 0:
  10.1 81.9 all-gather.8
  94.0 74.0 all-gather.4
  169.9 77.7 all-gather.6
  263.0 206.2 all-reduce.2
